TPU v7x, 256 devices: a whole 4x4x8 slice. The times are simulated.
256 devices in a mesh: grid: 32 (over z, y), var: 8 (over x, core).
Axes of the slice: x: 4, y: 4, z: 8, core: 2. Of those that a mesh axis runs over, the one named last changes fastest.
Arguments:
- data: bfloat16 [8, 1024, 49152], P('var', None, 'grid'), may hold values from -6 to 6
- area: float32 [49152], P('grid'), may hold values from 0.1 to 1
- eofs: bfloat16 [8, 49152, 128], P('var', 'grid'), may hold values from -0.02734375 to 0.02734375
- var_scale: float32 [8], P('var'), may hold values from 0.5 to 2
- recon_map: bfloat16 [8, 1024, 49152], P('var', None, 'grid'), may hold values from -0.1875 to 0.1875
Outputs:
- fields: bfloat16 [8, 1024, 49152], P('var', None, 'grid')
All inputs are finite; a program needn't handle non-finite values.
Results may differ from a plain program's by a relative error of at most 0.0057.
Values may be sent and summed in bfloat16 or wider, within the bound.
No kernel may reach another device: no remote copies, remote signals or barrier semaphores. Data moves between devices by JAX's collectives and lax.ppermute only.
A program may use at most 64 MiB of HBM per device.

v0:
```python
import jax
import jax.numpy as jnp
from jax import lax
from jax.sharding import PartitionSpec as P


def body(data, area, eofs, var_scale, recon_map):
    scaled = (area[:, None] * eofs[0].astype(jnp.float32)).astype(jnp.bfloat16)
    partial_comps = jnp.dot(data[0], scaled, preferred_element_type=jnp.float32)
    comps = lax.psum(partial_comps, "grid")
    joined_local = (var_scale[0] * comps).astype(jnp.bfloat16)
    patterns = recon_map[0]
    rebuilt = jnp.dot(
        lax.all_gather(joined_local, "var", axis=1, tiled=True),
        patterns,
        preferred_element_type=jnp.float32,
    )
    return rebuilt.astype(jnp.bfloat16)[None]


def solution(mesh):
    placed = (
        P("var", None, "grid"),
        P("grid"),
        P("var", "grid", None),
        P("var"),
        P("var", None, "grid"),
    )
    return jax.shard_map(
        body, mesh=mesh, in_specs=placed, out_specs=P("var", None, "grid"), check_vma=False
    )
```

profile of v0, /device:TPU:1, one launch (start us, length us, event | category | flops | bytes accessed | tf_op | source)
XLA Modules:
  0.0 204.4 jit_solution(12069375334948118248)
XLA Ops:
  6.5 0.0 copy-start
  6.5 0.0 all-reduce.2.cloned.1.call-start
  6.5 4.0 %fusion.4 = f32[1024,128]{1,0:T(8,128)} fusion(bf16[1,1024,1536]{2,1,0:T(8,128)(2,1)} %param.5, bf16[1,1536,128]{2,1,0:T(8,128)(2,1)} %param.7, f32[1536]{0:T(1024)} %param.6), kind=kOutput, calls=%fused_computation.5 | convolution fusion | flops 403243008 | bytes 4069376 | tf_op jit(solution)/shard_map/dot_general | solution.py:9
  10.6 0.0 all-reduce.2.cloned.1.call-update
  10.6 0.0 all-gather.2.cloned.1.call-start
  11.3 146.2 %all-reduce.2.cloned.1.call-done = f32[1024,128]{1,0:T(8,128)} async-done(((f32[1024,128]{1,0:T(8,128)}), f32[1024,128]{1,0:T(8,128)}) %all-reduce.2.cloned.1.call-update) | async-done | bytes 524304 | tf_op jit(solution)/shard_map/psum | solution.py:10
  157.5 1.8 multiply_convert_fusion.1
  159.3 0.0 all-gather.2.cloned.1.call-update
  159.3 31.9 %all-gather.2.cloned.1.call-done = bf16[1024,1024]{1,0:T(8,128)(2,1)} async-done(((bf16[1024,128]{1,0:T(8,128)(2,1)}), bf16[1024,1024]{1,0:T(8,128)(2,1)}) %all-gather.2.cloned.1.call-update) | async-done | bytes 2097168 | tf_op jit(solution)/shard_map/all_gather | solution.py:14
  191.2 0.0 copy-done
  191.2 6.3 %fusion = bf16[1,1024,1536]{2,1,0:T(8,128)(2,1)} fusion(bf16[1024,1024]{1,0:T(8,128)(2,1)} %all-gather.2.cloned.1.call-done, bf16[1,1024,1536]{2,1,0:T(8,128)(2,1)S(1)} %copy-done), kind=kOutput, calls=%fused_computation.1 | convolution fusion | flops 3222798336 | bytes 8388608 | tf_op jit(solution)/shard_map/dot_general | solution.py:13
Async XLA Ops:
  6.5 184.7 %copy-start = (bf16[1,1024,1536]{2,1,0:T(8,128)(2,1)S(1)}, bf16[1,1024,1536]{2,1,0:T(8,128)(2,1)}, u32[]{:S(2)}) copy-start(bf16[1,1024,1536]{2,1,0:T(8,128)(2,1)} %param.9) | copy-start | bytes 9437188
  6.5 151.0 %all-reduce.2.cloned.1.call-start = ((), (), s32[]{:S(2)}) async-start(), calls=%async_computation | async-start | bytes 1048576 | tf_op jit(solution)/shard_map/psum | solution.py:10
  10.6 180.6 %all-gather.2.cloned.1.call-start = ((), (), s32[]{:S(2)}) async-start(), calls=%async_computation.1 | async-start | bytes 2359296 | tf_op jit(solution)/shard_map/all_gather | solution.py:14
Sparse Core Ops, SparseCore 0:
  10.8 146.7 all-reduce.1
  159.5 31.6 all-gather.1
where the time goes:
time: 205 us; the launch traced here: 204 us
  waiting for transfers between devices  178 us (87%)
  between operations  14 us (7%)
  matrix products  10.4 us (5%)
    psum x1, waiting for transfers between devices, body(): comps = lax.psum(partial_comps, 'grid')  146 us
    all_gather x1, waiting for transfers between devices, body(): lax.all_gather(joined_local, 'var', axis=1, tiled=True)  31.9 us
    dot_general x1, matrix products, body(): jnp.dot(lax.all_gather(joined_local, 'var', axis=1, tiled=True), patterns...  6.35 us
  transfers between devices with their start and end apart: 2, of which 2 were waited for; matrix products, arithmetic and copies ran while one was open for 0% of the time, Pallas kernels for 0%

commit v1 on v0

--- a/solution.py
+++ b/solution.py
@@ -7,7 +7,7 @@
 def body(data, area, eofs, var_scale, recon_map):
     scaled = (area[:, None] * eofs[0].astype(jnp.float32)).astype(jnp.bfloat16)
     partial_comps = jnp.dot(data[0], scaled, preferred_element_type=jnp.float32)
-    comps = lax.psum(partial_comps, "grid")
+    comps = jnp.sum(lax.all_gather(partial_comps, "grid"), axis=0)
     joined_local = (var_scale[0] * comps).astype(jnp.bfloat16)
     patterns = recon_map[0]
     rebuilt = jnp.dot(

time: 205 us -> 224 us (1.093)
  local copies, waits for them, and re-layouts: 0.01 us -> 17.7 us
  other arithmetic: 1.77 us -> 11.6 us
  waiting for transfers between devices: 178 us -> 169 us
    psum x1 -> x0, waiting for transfers between devices: 146 us -> none  [body(): comps = lax.psum(partial_comps, 'grid')]
    all_gather x0 -> x1, waiting for transfers between devices: none -> 143 us  [body(): comps = jnp.sum(lax.all_gather(partial_comps, 'grid'), axis=0)]
    unnamed x2 -> x3, local copies, waits for them, and re-layouts: 0.01 us -> 17.7 us
    reduce_sum x0 -> x1, other arithmetic: none -> 9.79 us  [body(): comps = jnp.sum(lax.all_gather(partial_comps, 'grid'), axis=0)]
    all_gather x1, waiting for transfers between devices: 31.9 us -> 25.7 us  [body(): lax.all_gather(joined_local, 'var', axis=1, tiled=True)]
where the time goes in v1:
time: 224 us; the launch traced here: 223 us
  waiting for transfers between devices  169 us (75%)
  local copies, waits for them, and re-layouts  17.7 us (8%)
  between operations  14.1 us (6%)
  other arithmetic  11.6 us (5%)
  matrix products  11 us (5%)
    all_gather x1, waiting for transfers between devices, body(): comps = jnp.sum(lax.all_gather(partial_comps, 'grid'), axis=0)  143 us
    all_gather x1, waiting for transfers between devices, body(): lax.all_gather(joined_local, 'var', axis=1, tiled=True)  25.7 us
    unnamed x3, local copies, waits for them, and re-layouts  17.7 us
    reduce_sum x1, other arithmetic, body(): comps = jnp.sum(lax.all_gather(partial_comps, 'grid'), axis=0)  9.79 us
    dot_general x1, matrix products, body(): jnp.dot(lax.all_gather(joined_local, 'var', axis=1, tiled=True), patterns...  6.5 us
  transfers between devices with their start and end apart: 2, of which 2 were waited for; matrix products, arithmetic and copies ran while one was open for 0% of the time, Pallas kernels for 0%

profile of v1, /device:TPU:1, one launch (start us, length us, event | category | flops | bytes accessed | tf_op | source)
XLA Modules:
  0.0 223.5 jit_solution(17220732359094920945)
XLA Ops:
  6.5 0.0 copy-start
  6.5 0.0 all-gather.6.cloned.1.call-start
  6.5 4.5 %fusion.4 = f32[1024,128]{0,1:T(8,128)} fusion(bf16[1,1024,1536]{2,1,0:T(8,128)(2,1)} %param.5, bf16[1,1536,128]{2,1,0:T(8,128)(2,1)} %param.7, f32[1536]{0:T(1024)} %param.6), kind=kOutput, calls=%fused_computation.6 | convolution fusion | flops 403243008 | bytes 4069376 | tf_op jit(solution)/shard_map/dot_general | solution.py:9
  11.0 0.0 all-gather.6.cloned.1.call-update
  11.0 0.0 all-gather.4.cloned.1.call-start
  11.7 143.4 %all-gather.6.cloned.1.call-done = f32[32768,128]{0,1:T(8,128)} async-done(((f32[1024,128]{0,1:T(8,128)}), f32[32768,128]{0,1:T(8,128)}) %all-gather.6.cloned.1.call-update) | async-done | bytes 16777232 | tf_op jit(solution)/shard_map/all_gather | solution.py:10
  155.2 17.7 %copy.6 = f32[16,8,32,1024]{3,2,1,0:T(8,128)} copy(f32[16,8,32,1024]{3,1,2,0:T(8,128)} %bitcast.23) | data formatting | bytes 33554432
  172.8 9.8 %bitcast_reduce_fusion = f32[1024,128]{0,1:T(8,128)} fusion(f32[16,8,32,1024]{3,2,1,0:T(8,128)} %copy.6), kind=kLoop, calls=%fused_computation | loop fusion | flops 4063232 | bytes 17301504 | tf_op jit(solution)/shard_map/reduce_sum | solution.py:10
  182.6 1.8 multiply_convert_fusion.1
  184.4 0.0 all-gather.4.cloned.1.call-update
  184.4 25.7 %all-gather.4.cloned.1.call-done = bf16[1024,1024]{0,1:T(8,128)(2,1)} async-done(((bf16[1024,128]{0,1:T(8,128)(2,1)}), bf16[1024,1024]{0,1:T(8,128)(2,1)}) %all-gather.4.cloned.1.call-update) | async-done | bytes 2097168 | tf_op jit(solution)/shard_map/all_gather | solution.py:14
  210.1 0.0 copy-done
  210.1 6.5 %fusion = bf16[1,1024,1536]{2,1,0:T(8,128)(2,1)} fusion(bf16[1024,1024]{0,1:T(8,128)(2,1)} %all-gather.4.cloned.1.call-done, bf16[1,1024,1536]{2,1,0:T(8,128)(2,1)S(1)} %copy-done), kind=kOutput, calls=%fused_computation.2 | convolution fusion | flops 3222798336 | bytes 8388608 | tf_op jit(solution)/shard_map/dot_general | solution.py:13
Async XLA Ops:
  6.5 203.6 %copy-start = (bf16[1,1024,1536]{2,1,0:T(8,128)(2,1)S(1)}, bf16[1,1024,1536]{2,1,0:T(8,128)(2,1)}, u32[]{:S(2)}) copy-start(bf16[1,1024,1536]{2,1,0:T(8,128)(2,1)} %param.9) | copy-start | bytes 9437188
  6.5 148.6 %all-gather.6.cloned.1.call-start = ((), (), s32[]{:S(2)}) async-start(), calls=%async_computation.1 | async-start | bytes 17301504 | tf_op jit(solution)/shard_map/all_gather | solution.py:10
  11.0 199.1 %all-gather.4.cloned.1.call-start = ((), (), s32[]{:S(2)}) async-start(), calls=%async_computation | async-start | bytes 2359296 | tf_op jit(solution)/shard_map/all_gather | solution.py:14
Sparse Core Ops, SparseCore 0:
  11.2 143.9 all-gather.5
  184.6 25.5 all-gather.3
